TPU v7x, 32 devices: a whole 2x2x4 slice. The times are simulated.
32 devices in a mesh: dp: 8 (over y, x, core), pencil: 4 (over z).
Axes of the slice: x: 2, y: 2, z: 4, core: 2. Of those that a mesh axis runs over, the one named last changes fastest.
Arguments:
- field: bfloat16 [8, 64, 64, 64, 128], P('dp', 'pencil'), may hold values from -6 to 6
- cotangent: bfloat16 [8, 64, 64, 64, 128], P('dp', 'pencil'), may hold values from -6 to 6
- w_spec: bfloat16 [16, 16, 16, 64, 128], P('dp', 'pencil'), may hold values from -6 to 6
- w_local: bfloat16 [64, 64], replicated, may hold values from -0.75 to 0.75
Outputs:
- grad_field: bfloat16 [8, 64, 64, 64, 128], P('dp', 'pencil')
- grad_w: float32 [16, 16, 16, 64, 128], P('dp', 'pencil')
All inputs are finite; a program needn't handle non-finite values.
Results may differ from a plain program's by a relative error of at most 0.02.
Values may be sent and summed in bfloat16 or wider, within the bound.
A program may use at most 192 MiB of HBM per device.

v0:
```python
import math

import jax
import jax.numpy as jnp
from jax import lax
from jax.sharding import PartitionSpec as P

NX = 64
NY = 64
NZ = 128
CH = 64
MX = 16
MY = 16
MZ = 16


HIGHEST = lax.Precision.HIGHEST


def phase_pair(length, mode_count, signed):
    position = jnp.arange(length, dtype=jnp.int32)
    indices = jnp.arange(mode_count, dtype=jnp.int32)
    frequency = (
        jnp.where(indices < mode_count // 2, indices, indices - mode_count) if signed else indices
    )
    product = jnp.mod(position[:, None] * frequency[None, :], length).astype(jnp.float32)
    angles = product * (2.0 * math.pi / length)
    return (jnp.cos(angles), jnp.sin(angles))


def grid_tables():
    cos_x, sin_x = phase_pair(NX, MX, True)
    cos_y, sin_y = phase_pair(NY, MY, True)
    cos_z, sin_z = phase_pair(NZ, MZ, False)
    forward_z = jnp.concatenate([cos_z, -sin_z], 1).astype(jnp.bfloat16)
    weight_z = jnp.where(jnp.arange(MZ, dtype=jnp.int32) == 0, 1.0, 2.0).astype(jnp.float32) / (
        NX * NY * NZ
    )
    inverse_z = jnp.concatenate([cos_z * weight_z, -sin_z * weight_z], 1).T
    adjoint_z = jnp.concatenate([cos_z, -sin_z], 1).T
    spectrum_scale = jnp.concatenate([weight_z, weight_z])
    return (cos_x, sin_x, cos_y, sin_y, forward_z, inverse_z, adjoint_z, spectrum_scale)


def rotate_half(values):
    middle = values.shape[-1] // 2
    return jnp.concatenate([values[..., middle:], -values[..., :middle]], -1)


def along_y(values, cosines, sine_table, inverse):
    pattern = "xjck,yj->xyck" if inverse else "xyck,yj->xjck"
    factor = -1.0 if inverse else 1.0
    direct = jnp.einsum(pattern, values, cosines, precision=HIGHEST)
    turned = jnp.einsum(pattern, rotate_half(values), sine_table, precision=HIGHEST)
    return direct + factor * turned


def along_x(values, cosines, sine_table, inverse):
    pattern = "jbck,xj->xbck" if inverse else "xbck,xj->jbck"
    factor = -1.0 if inverse else 1.0
    direct = jnp.einsum(pattern, values, cosines, precision=HIGHEST)
    turned = jnp.einsum(pattern, rotate_half(values), sine_table, precision=HIGHEST)
    return direct + factor * turned


def z_forward(field_in, matrix):
    shape_in = field_in.shape
    product = jnp.dot(
        field_in.reshape(-1, shape_in[-1]), matrix, preferred_element_type=jnp.float32
    )
    return product.reshape(shape_in[:-1] + (matrix.shape[1],))


def z_back(values, matrix):
    shape_in = values.shape
    product = jnp.dot(
        values.reshape(-1, shape_in[-1]),
        matrix,
        precision=HIGHEST,
        preferred_element_type=jnp.float32,
    )
    return product.reshape(shape_in[:-1] + (matrix.shape[1],))


def gelu_slope(pre):
    normal_cdf = 0.5 * (1.0 + lax.erf(pre * (1.0 / math.sqrt(2.0))))
    return normal_cdf + pre * jnp.exp(-0.5 * pre * pre) * (1.0 / math.sqrt(2.0 * math.pi))


def apply_modes(coeffs, weights):
    real_part = coeffs[..., :MZ]
    imag_part = coeffs[..., MZ:]
    from_real = jnp.einsum(
        "sabik,abkio->sabok", real_part, weights, preferred_element_type=jnp.float32
    )
    from_imag = jnp.einsum(
        "sabik,abkio->sabok", imag_part, weights, preferred_element_type=jnp.float32
    )
    out_real = from_real[:, :, :, :CH] - from_imag[:, :, :, CH:]
    out_imag = from_real[:, :, :, CH:] + from_imag[:, :, :, :CH]
    return jnp.concatenate([out_real, out_imag], -1)


def paired(g_modes):
    g_real = g_modes[..., :MZ]
    g_imag = g_modes[..., MZ:]
    return (jnp.concatenate([g_real, g_imag], -2), jnp.concatenate([g_imag, -g_real], -2))


def adjoint_modes(g_modes, weights):
    paired_one, paired_two = paired(g_modes)
    back_real = jnp.einsum(
        "abkio,sabok->sabik", weights, paired_one, preferred_element_type=jnp.float32
    )
    back_imag = jnp.einsum(
        "abkio,sabok->sabik", weights, paired_two, preferred_element_type=jnp.float32
    )
    return jnp.concatenate([back_real, back_imag], -1)


def mode_grads(u_modes, g_modes):
    paired_one, paired_two = paired(g_modes)
    from_real = jnp.einsum(
        "sabik,sabok->abkio", u_modes[..., :MZ], paired_one, preferred_element_type=jnp.float32
    )
    from_imag = jnp.einsum(
        "sabik,sabok->abkio", u_modes[..., MZ:], paired_two, preferred_element_type=jnp.float32
    )
    return from_real + from_imag


def to_modes(field_in, tables):
    cos_x, sin_x, cos_y, sin_y, forward_z = (tables[0], tables[1], tables[2], tables[3], tables[4])
    sectioned = along_y(z_forward(field_in, forward_z), cos_y, sin_y, False)
    arrived = lax.all_to_all(
        sectioned.astype(jnp.bfloat16), "pencil", split_axis=1, concat_axis=0, tiled=True
    ).astype(sectioned.dtype)
    return along_x(arrived, cos_x, sin_x, False)


def to_grid(coeffs, tables, matrix):
    cos_x, sin_x, cos_y, sin_y = (tables[0], tables[1], tables[2], tables[3])
    sectioned = along_x(coeffs, cos_x, sin_x, True)
    arrived = lax.all_to_all(
        sectioned.astype(jnp.bfloat16), "pencil", split_axis=0, concat_axis=1, tiled=True
    ).astype(sectioned.dtype)
    return z_back(along_y(arrived, cos_y, sin_y, True), matrix)


def to_owner(coeffs):
    return lax.all_to_all(coeffs[None], "dp", split_axis=1, concat_axis=0, tiled=True)


def from_owner(coeffs):
    return lax.all_to_all(
        coeffs.astype(jnp.bfloat16), "dp", split_axis=0, concat_axis=1, tiled=True
    ).astype(coeffs.dtype)[0]


def body(field, cotangent, w_spec, w_local):
    tables = grid_tables()
    inverse_z, adjoint_z, spectrum_scale = (tables[5], tables[6], tables[7])
    sample = field[0]
    target = cotangent[0]
    u_modes = to_modes(sample, tables).astype(jnp.bfloat16)
    u_sent = to_owner(u_modes)
    v_modes = from_owner(apply_modes(u_sent, w_spec))
    values = to_grid(v_modes, tables, inverse_z)
    bypass = jnp.einsum("xycz,co->xyoz", sample, w_local, preferred_element_type=jnp.float32)
    slope_in = (target.astype(jnp.float32) * gelu_slope(values + bypass)).astype(jnp.bfloat16)
    g_modes = (to_modes(slope_in, tables) * spectrum_scale).astype(jnp.bfloat16)
    g_sent = to_owner(g_modes)
    grad_w = mode_grads(u_sent, g_sent)
    back_modes = from_owner(adjoint_modes(g_sent, w_spec))
    spread = jnp.einsum("xyoz,co->xycz", slope_in, w_local, preferred_element_type=jnp.float32)
    grad_sample = (to_grid(back_modes, tables, adjoint_z) + spread).astype(jnp.bfloat16)
    return (grad_sample[None], grad_w)


def solution(mesh):
    placed = (
        P("dp", "pencil", None, None, None),
        P("dp", "pencil", None, None, None),
        P("dp", "pencil", None, None, None),
        P(),
    )
    return jax.shard_map(
        body,
        mesh=mesh,
        in_specs=placed,
        out_specs=(P("dp", "pencil", None, None, None), P("dp", "pencil", None, None, None)),
        check_vma=False,
    )
```

profile of v0, /device:TPU:1, one launch (start us, length us, event | category | flops | bytes accessed | tf_op | source)
XLA Modules:
  0.0 624.4 jit_solution(11396002649751547669)
XLA Ops:
  0.7 15.0 %convolution_bitcast_fusion = f32[65536,32]{0,1:T(8,128)} fusion(bf16[65536,128]{1,0:T(8,128)(2,1)} %bitcast.173, f32[128,16]{0,1:T(8,128)S(1)} %get-tuple-element.28, f32[128,16]{0,1:T(8,128)S(1)} %get-tuple-element.29), kind=kOutput, calls=%fused_computation | convolution fusion | flops 536887296 | bytes 25182208 | tf_op jit(solution)/shard_map/dot_general | solution.py:68
  15.7 12.7 %reshape.60 = f32[16,64,64,32]{2,1,0,3:T(8,128)} reshape(f32[65536,32]{0,1:T(8,128)} %convolution_bitcast_fusion) | data formatting | bytes 16777216 | tf_op jit(solution)/shard_map/reshape | solution.py:71
  28.4 13.6 %fusion.227 = (f32[16,64,64,16]{2,1,3,0:T(8,128)}, f32[16,64,64,16]{2,1,3,0:T(8,128)}) fusion(f32[16,64,64,32]{2,1,0,3:T(8,128)} %reshape.60), kind=kLoop, calls=%fused_computation.242 | loop fusion | flops 1048576 | bytes 16777216 | tf_op jit(solution)/shard_map/slice | solution.py:47
  42.0 14.0 %fusion.8 = f32[16,16,64,32]{2,0,3,1:T(8,128)} fusion(f32[16,64,64,16]{2,1,3,0:T(8,128)} %get-tuple-element.5, f32[16,64,64,16]{2,1,3,0:T(8,128)} %get-tuple-element.4, s32[16]{0:T(128)S(1)} %compare_select_fusion), kind=kOutput, calls=%fused_computation.12 | convolution fusion | flops 404764672 | bytes 10485824 | tf_op jit(solution)/shard_map/xyck,yj->xjck/dot_general | solution.py:54
  56.0 10.0 %fusion.45 = bf16[16,16,64,32]{2,1,3,0:T(8,128)(2,1)S(1)} fusion(f32[16,16,64,32]{2,0,3,1:T(8,128)} %fusion.8, s32[16]{0:T(128)S(1)} %compare_select_fusion, f32[16,64,64,32]{2,1,0,3:T(8,128)S(1)} %bitcast.172), kind=kOutput, calls=%fused_computation.61 | convolution fusion | flops 403716096 | bytes 11534400 | tf_op jit(solution)/shard_map/xyck,yj->xjck/dot_general | solution.py:53
  67.9 3.4 reshape.69
  71.3 30.2 %all_to_all.114 = bf16[4,2,65536]{2,1,0:T(2,128)(2,1)} all-to-all(bf16[4,2,65536]{2,1,0:T(2,128)(2,1)S(1)} %reshape.69), channel_id=1, replica_groups=mesh['dp'=8,'pencil'=4] {'pencil'}, dimensions={0} | all-to-all | bytes 2097152 | tf_op jit(solution)/shard_map/all_to_all | solution.py:135
  101.5 4.3 reshape.70
  105.8 2.4 copy.68
  110.6 2.3 fusion.64
  113.4 11.0 %all_to_all.115 = bf16[8,2,8192]{2,1,0:T(2,128)(2,1)S(1)} all-to-all(bf16[8,2,8192]{2,1,0:T(2,128)(2,1)S(1)} %reshape.71), channel_id=1, replica_groups=mesh['dp'=8,'pencil'=4] {'dp'}, dimensions={0} | all-to-all | bytes 524288 | tf_op jit(solution)/shard_map/all_to_all | solution.py:151
  127.2 9.3 %all_to_all.116 = bf16[8,2,8192]{2,1,0:T(2,128)(2,1)S(1)} all-to-all(bf16[8,2,8192]{2,1,0:T(2,128)(2,1)S(1)} %reshape.73), channel_id=1, replica_groups=mesh['dp'=8,'pencil'=4] {'dp'}, dimensions={0} | all-to-all | bytes 524288 | tf_op jit(solution)/shard_map/all_to_all | solution.py:155
  139.3 4.1 add_convert_fusion.2
  143.4 2.7 copy.155
  146.1 4.4 reshape.75
  150.5 3.9 all-to-all-start.3
  154.5 25.2 %all-to-all-done.3 = bf16[4,2,65536]{2,1,0:T(2,128)(2,1)S(1)} async-done(((bf16[4,2,65536]{2,1,0:T(2,128)(2,1)}), bf16[4,2,65536]{2,1,0:T(2,128)(2,1)S(1)}, u32[]{:S(2)}, u32[]{:S(2)}) %all-to-all-start.3) | async-done | bytes 1048608 | tf_op jit(solution)/shard_map/all_to_all | solution.py:144
  179.6 2.7 reshape.76
  184.2 10.6 %fusion.43 = f32[64,16,64,32]{2,0,3,1:T(8,128)} fusion(bf16[16,16,64,32]{2,3,1,0:T(8,128)(2,1)S(1)} %bitcast.176, s32[16]{0:T(128)S(1)} %compare_select_fusion), kind=kOutput, calls=%fused_computation.59 | convolution fusion | flops 402667520 | bytes 9437248 | tf_op jit(solution)/shard_map/xjck,yj->xyck/dot_general | solution.py:53
  195.9 19.0 %add_bitcast_fusion.1 = f32[16,64,64,32]{2,1,3,0:T(8,128)} fusion(f32[64,16,64,32]{2,0,3,1:T(8,128)} %fusion.43, f32[16,16,64,16]{2,1,3,0:T(8,128)S(1)} %get-tuple-element.11, f32[16,16,64,16]{2,1,3,0:T(8,128)S(1)} %get-tuple-element.10, s32[16]{0:T(128)S(1)} %compare_select_fusion), kind=kOutput, calls=%fused_computation.28 | convolution fusion | flops 407386112 | bytes 18874432 | tf_op jit(solution)/shard_map/xjck,yj->xyck/dot_general | solution.py:54
  214.9 65.2 %fusion.20 = f32[16,64,64,128]{3,2,1,0:T(8,128)} fusion(f32[16,64,64,32]{2,1,3,0:T(8,128)} %add_bitcast_fusion.1, f32[128,16]{0,1:T(8,128)S(1)} %get-tuple-element.27, f32[128,16]{0,1:T(8,128)S(1)} %get-tuple-element.26), kind=kOutput, calls=%fused_computation.25 | convolution fusion | flops 3221229568 | bytes 41959424 | tf_op jit(solution)/shard_map/dot_general | solution.py:76
  280.2 31.4 %fusion.5 = bf16[16,64,64,128]{3,2,1,0:T(8,128)(2,1)} fusion(f32[16,64,64,128]{3,2,1,0:T(8,128)} %fusion.20, bf16[1,16,64,64,128]{4,3,2,1,0:T(8,128)(2,1)} %param.5, bf16[1,16,64,64,128]{4,3,2,1,0:T(8,128)(2,1)} %param.4, bf16[64,64]{1,0:T(8,128)(2,1)S(1)} %copy-done.7), kind=kOutput, calls=%fused_computation.7 | convolution fusion | flops 1174405120 | bytes 83894272 | tf_op jit(solution)/shard_map/xycz,co->xyoz/dot_general | solution.py:169
  311.6 19.4 %fusion.98 = f32[16,64,64,32]{2,3,1,0:T(8,128)S(1)} fusion(bf16[16,64,64,128]{3,2,1,0:T(8,128)(2,1)} %fusion.5, f32[128,16]{0,1:T(8,128)S(1)} %get-tuple-element.28, f32[128,16]{0,1:T(8,128)S(1)} %get-tuple-element.29), kind=kOutput, calls=%fused_computation.122 | convolution fusion | flops 536887296 | bytes 25182208 | tf_op jit(solution)/shard_map/dot_general | solution.py:68
  331.0 6.8 %fusion.226 = (f32[16,64,64,16]{2,3,1,0:T(8,128)}, f32[16,64,64,16]{2,3,1,0:T(8,128)}) fusion(f32[16,64,64,32]{2,3,1,0:T(8,128)S(1)} %fusion.98), kind=kLoop, calls=%fused_computation.241 | loop fusion | flops 1048576 | bytes 16777216 | tf_op jit(solution)/shard_map/slice | solution.py:47
  337.7 12.0 %pad_maximum_fusion = f32[16,64,64,32]{2,3,1,0:T(8,128)} fusion(f32[16,64,64,16]{2,3,1,0:T(8,128)} %get-tuple-element.3, f32[16,64,64,16]{2,3,1,0:T(8,128)} %get-tuple-element.2), kind=kLoop, calls=%fused_computation.16 | loop fusion | flops 2097152 | bytes 16777216 | tf_op jit(solution)/shard_map/concatenate | solution.py:47
  349.8 23.7 %fusion.16 = f32[16,16,64,32]{2,0,3,1:T(8,128)} fusion(f32[16,64,64,32]{2,3,1,0:T(8,128)} %pad_maximum_fusion, s32[16]{0:T(128)S(1)} %compare_select_fusion), kind=kOutput, calls=%fused_computation.21 | convolution fusion | flops 402667520 | bytes 10485824 | tf_op jit(solution)/shard_map/xyck,yj->xjck/dot_general | solution.py:54
  373.5 17.0 %fusion.38 = bf16[16,16,64,32]{2,1,3,0:T(8,128)(2,1)S(1)} fusion(f32[16,16,64,32]{2,0,3,1:T(8,128)} %fusion.16, f32[16,64,64,32]{2,3,1,0:T(8,128)S(1)} %fusion.98, s32[16]{0:T(128)S(1)} %compare_select_fusion), kind=kOutput, calls=%fused_computation.50 | convolution fusion | flops 403716096 | bytes 11534400 | tf_op jit(solution)/shard_map/xyck,yj->xjck/dot_general | solution.py:53
  392.3 4.4 reshape.77
  396.6 3.7 all-to-all-start.4
  400.5 25.2 %all-to-all-done.4 = bf16[4,2,65536]{2,1,0:T(2,128)(2,1)S(1)} async-done(((bf16[4,2,65536]{2,1,0:T(2,128)(2,1)}), bf16[4,2,65536]{2,1,0:T(2,128)(2,1)S(1)}, u32[]{:S(2)}, u32[]{:S(2)}) %all-to-all-start.4) | async-done | bytes 1048608 | tf_op jit(solution)/shard_map/all_to_all | solution.py:135
  425.6 2.7 reshape.78
  428.3 2.4 copy.84
  433.1 2.3 fusion.61
  435.9 9.5 %all_to_all.117 = bf16[8,2,8192]{2,1,0:T(2,128)(2,1)S(1)} all-to-all(bf16[8,2,8192]{2,1,0:T(2,128)(2,1)S(1)} %reshape.79), channel_id=1, replica_groups=mesh['dp'=8,'pencil'=4] {'dp'}, dimensions={0} | all-to-all | bytes 524288 | tf_op jit(solution)/shard_map/all_to_all | solution.py:151
  449.4 9.3 %all_to_all.118 = bf16[8,2,8192]{2,1,0:T(2,128)(2,1)S(1)} all-to-all(bf16[8,2,8192]{2,1,0:T(2,128)(2,1)S(1)} %reshape.81), channel_id=1, replica_groups=mesh['dp'=8,'pencil'=4] {'dp'}, dimensions={0} | all-to-all | bytes 524288 | tf_op jit(solution)/shard_map/all_to_all | solution.py:155
  459.0 2.0 fusion.77
  461.4 4.1 add_convert_fusion
  465.5 2.7 copy.153
  468.2 4.4 reshape.83
  472.6 4.0 all-to-all-start.7
  476.6 2.0 fusion.83
  478.6 2.9 convolution_add_fusion
  481.5 20.3 %all-to-all-done.7 = bf16[4,2,65536]{2,1,0:T(2,128)(2,1)S(1)} async-done(((bf16[4,2,65536]{2,1,0:T(2,128)(2,1)}), bf16[4,2,65536]{2,1,0:T(2,128)(2,1)S(1)}, u32[]{:S(2)}, u32[]{:S(2)}) %all-to-all-start.7) | async-done | bytes 1048608 | tf_op jit(solution)/shard_map/all_to_all | solution.py:144
  501.8 2.7 reshape.84
  506.4 10.6 %fusion.41 = f32[64,16,64,32]{2,0,3,1:T(8,128)} fusion(bf16[16,16,64,32]{2,3,1,0:T(8,128)(2,1)S(1)} %bitcast.178, s32[16]{0:T(128)S(1)} %compare_select_fusion), kind=kOutput, calls=%fused_computation.56 | convolution fusion | flops 402667520 | bytes 9437248 | tf_op jit(solution)/shard_map/xjck,yj->xyck/dot_general | solution.py:53
  518.1 19.0 %add_bitcast_fusion = f32[16,64,64,32]{2,1,3,0:T(8,128)} fusion(f32[64,16,64,32]{2,0,3,1:T(8,128)} %fusion.41, f32[16,16,64,16]{2,1,3,0:T(8,128)S(1)} %get-tuple-element.7, f32[16,16,64,16]{2,1,3,0:T(8,128)S(1)} %get-tuple-element.6, s32[16]{0:T(128)S(1)} %compare_select_fusion), kind=kOutput, calls=%fused_computation.27 | convolution fusion | flops 407386112 | bytes 18874432 | tf_op jit(solution)/shard_map/xjck,yj->xyck/dot_general | solution.py:54
  537.1 64.8 %fusion.14 = f32[16,64,64,128]{3,2,1,0:T(8,128)} fusion(f32[16,64,64,32]{2,1,3,0:T(8,128)} %add_bitcast_fusion, f32[128,16]{0,1:T(8,128)S(1)} %get-tuple-element.28, f32[128,16]{0,1:T(8,128)S(1)} %get-tuple-element.29), kind=kOutput, calls=%fused_computation.19 | convolution fusion | flops 3221229568 | bytes 41959424 | tf_op jit(solution)/shard_map/dot_general | solution.py:76
  602.0 22.2 %fusion.7 = bf16[1,16,64,64,128]{4,3,2,1,0:T(8,128)(2,1)} fusion(f32[16,64,64,128]{3,2,1,0:T(8,128)} %fusion.14, bf16[16,64,64,128]{3,2,1,0:T(8,128)(2,1)} %fusion.5, bf16[64,64]{1,0:T(8,128)(2,1)S(1)} %copy-done.7), kind=kOutput, calls=%fused_computation.11 | convolution fusion | flops 1090519040 | bytes 67117056 | tf_op jit(solution)/shard_map/xyoz,co->xycz/dot_general | solution.py:175
  (72 shorter events, 25.9 us)
Async XLA Ops:
  0.6 124.2 %copy-start = (bf16[2,4,16,64,128]{4,3,2,1,0:T(8,128)(2,1)S(1)}, bf16[2,4,16,64,128]{4,3,2,1,0:T(8,128)(2,1)}, u32[]{:S(2)}) copy-start(bf16[2,4,16,64,128]{4,3,2,1,0:T(8,128)(2,1)} %param.6) | copy-start | bytes 6291460
  28.4 27.6 %slice-start = ((s8[16777216]{0:T(1024)(128)(4,1)}), s8[4194304]{0:T(1024)(128)(4,1)S(1)}, s32[]{:S(2)}) async-start(s8[16777216]{0:T(1024)(128)(4,1)} %bitcast.171), calls=%async_computation.8 | async-start | bytes 8388608
  28.4 27.6 %slice-start.1 = ((s8[16777216]{0:T(1024)(128)(4,1)}), s8[4194304]{0:T(1024)(128)(4,1)S(1)}, s32[]{:S(2)}) async-start(s8[16777216]{0:T(1024)(128)(4,1)} %bitcast.171), calls=%async_computation.9 | async-start | bytes 8388608
  28.4 27.6 %slice-start.2 = ((s8[16777216]{0:T(1024)(128)(4,1)}), s8[4194304]{0:T(1024)(128)(4,1)S(1)}, s32[]{:S(2)}) async-start(s8[16777216]{0:T(1024)(128)(4,1)} %bitcast.171), calls=%async_computation.10 | async-start | bytes 8388608
  42.0 14.0 %slice-start.3 = ((s8[16777216]{0:T(1024)(128)(4,1)}), s8[4194304]{0:T(1024)(128)(4,1)S(1)}, s32[]{:S(2)}) async-start(s8[16777216]{0:T(1024)(128)(4,1)} %bitcast.171), calls=%async_computation.11 | async-start | bytes 8388608
  124.8 0.7 copy-start.4
  124.8 0.8 copy-start.6
  150.5 29.2 %all-to-all-start.3 = ((bf16[4,2,65536]{2,1,0:T(2,128)(2,1)}), bf16[4,2,65536]{2,1,0:T(2,128)(2,1)S(1)}, u32[]{:S(2)}, u32[]{:S(2)}) async-start(bf16[4,2,65536]{2,1,0:T(2,128)(2,1)} %reshape.75), calls=%async_computation.3 | async-start | bytes 2097152 | tf_op jit(solution)/shard_map/all_to_all | solution.py:144
  214.9 65.2 %copy-start.7 = (bf16[64,64]{1,0:T(8,128)(2,1)S(1)}, bf16[64,64]{1,0:T(8,128)(2,1)}, u32[]{:S(2)}) copy-start(bf16[64,64]{1,0:T(8,128)(2,1)} %param.7) | copy-start | bytes 24580
  396.6 29.0 %all-to-all-start.4 = ((bf16[4,2,65536]{2,1,0:T(2,128)(2,1)}), bf16[4,2,65536]{2,1,0:T(2,128)(2,1)S(1)}, u32[]{:S(2)}, u32[]{:S(2)}) async-start(bf16[4,2,65536]{2,1,0:T(2,128)(2,1)} %reshape.77), calls=%async_computation.4 | async-start | bytes 2097152 | tf_op jit(solution)/shard_map/all_to_all | solution.py:135
  446.0 2.9 copy-start.1
  446.0 2.9 copy-start.3
  472.6 29.2 %all-to-all-start.7 = ((bf16[4,2,65536]{2,1,0:T(2,128)(2,1)}), bf16[4,2,65536]{2,1,0:T(2,128)(2,1)S(1)}, u32[]{:S(2)}, u32[]{:S(2)}) async-start(bf16[4,2,65536]{2,1,0:T(2,128)(2,1)} %reshape.83), calls=%async_computation.7 | async-start | bytes 2097152 | tf_op jit(solution)/shard_map/all_to_all | solution.py:144
  476.6 2.0 copy-start.2
  476.6 2.0 copy-start.5
where the time goes:
time: 630 us; the launch traced here: 624 us
  matrix products  370 us (59%)
  waiting for transfers between devices  70.6 us (11%)
  blocking collectives  69.3 us (11%)
  local copies, waits for them, and re-layouts  63 us (10%)
  other arithmetic  38.9 us (6%)
  starting transfers between devices  11.6 us (2%)
    dot_general x2, matrix products, z_back(): jnp.dot(values.reshape(-1, shape_in[-1]), matrix, precision=HIGHEST, pref...  130 us
    dot_general x4, matrix products, along_y(): jnp.einsum(pattern, rotate_half(values), sine_table, precision=HIGHEST)  75.8 us
    dot_general x4, matrix products, along_y(): direct = jnp.einsum(pattern, values, cosines, precision=HIGHEST)  48.2 us
    all_to_all x2, waiting for transfers between devices, to_grid(): lax.all_to_all(sectioned.astype(jnp.bfloat16), 'pencil', split_axis=0, co...  45.4 us
    dot_general x2, matrix products, z_forward(): jnp.dot(field_in.reshape(-1, shape_in[-1]), matrix, preferred_element_typ...  34.4 us
    unnamed x41, local copies, waits for them, and re-layouts  32 us
    dot_general x1, matrix products, body(): jnp.einsum('xycz,co->xyoz', sample, w_local, preferred_element_type=jnp.f...  31.4 us
    all_to_all x1, blocking collectives, to_modes(): lax.all_to_all(sectioned.astype(jnp.bfloat16), 'pencil', split_axis=1, co...  30.2 us
  transfers between devices with their start and end apart: 3, of which 3 were waited for; matrix products, arithmetic and copies ran while one was open for 1% of the time, Pallas kernels for 0%

commit v1 on v0

v1 whole, which is shorter than its diff:
```python
import functools
import math

import jax
import jax.numpy as jnp
import numpy as np
from jax import lax
from jax.experimental import pallas as pl
from jax.experimental.pallas import tpu as pltpu
from jax.sharding import PartitionSpec as P

BF16 = jnp.bfloat16
F32 = jnp.float32
ROWS = 16
NXB = 2
YB = 4
VMEM = 64 * 1000 * 1024


def waves(length, count, signed):
    index = np.arange(count)
    freq = np.where(index < count // 2, index, index - count) if signed else index
    angle = 2.0 * math.pi * ((np.arange(length)[:, None] * freq[None, :]) % length) / length
    return np.cos(angle), np.sin(angle)


def kron_rows(matrix):
    return np.kron(matrix, np.eye(ROWS))


def const(array):
    return jnp.asarray(np.asarray(array, np.float32), BF16)


def make_tables(nx, ny, nz, groups, mx, my, mz, pencils):
    cx, sx = waves(nx, mx, True)
    cy, sy = waves(ny, my, True)
    cz, sz = waves(nz, mz, False)
    eye_g = np.eye(groups)
    plain = np.concatenate([cz, -sz], 1)
    turned = np.concatenate([-sz, -cz], 1)
    z_fwd = np.concatenate([np.kron(eye_g, plain), np.kron(eye_g, turned)], 1)
    weight = np.where(np.arange(mz) == 0, 1.0, 2.0) / (nx * ny * nz)
    z_inv = np.kron(eye_g, np.concatenate([cz * weight, -sz * weight], 1).T)
    z_adj = np.kron(eye_g, plain.T)
    half = np.eye(mz)
    zero = np.zeros((mz, mz))
    turn = np.kron(eye_g, np.block([[zero, -half], [half, zero]]))
    y_fwd = np.concatenate([kron_rows(cy.T), kron_rows(sy.T)], 1)
    y_inv = np.concatenate([kron_rows(cy), -kron_rows(sy)], 1)
    own = nx // pencils
    x_fwd, x_inv = [], []
    for q in range(pencils):
        c, s = cx[q * own : (q + 1) * own], sx[q * own : (q + 1) * own]
        x_fwd.append(np.concatenate([kron_rows(c.T), kron_rows(s.T)], 1))
        x_inv.append(np.concatenate([kron_rows(c), -kron_rows(s)], 1))
    scale = np.tile(np.concatenate([weight, weight]), groups)
    return dict(
        z_fwd=const(z_fwd),
        z_inv=const(z_inv),
        z_adj=const(z_adj),
        turn=const(turn),
        y_fwd=const(y_fwd),
        y_inv=const(y_inv),
        x_fwd=const(np.stack(x_fwd)),
        x_inv=const(np.stack(x_inv)),
        scale=jnp.asarray(scale, F32),
    )


def mm(a, b):
    return jnp.dot(a, b, preferred_element_type=F32)


def forward_zy(src, z_fwd, y_fwd, sections, step):
    nxb, ny, ch, nz = src.shape
    groups = ch // ROWS
    lanes = z_fwd.shape[1] // 2
    plain, turned = [], []
    for x in range(nxb):
        wide = jnp.concatenate(
            [src[x, :, g * ROWS : (g + 1) * ROWS, :].reshape(ny * ROWS, nz) for g in range(groups)], 1
        )
        spectral = mm(wide, z_fwd[...]).astype(BF16)
        plain.append(spectral[:, :lanes])
        turned.append(spectral[:, lanes:])
    stacked = jnp.concatenate([jnp.concatenate(plain, 1), jnp.concatenate(turned, 1)], 0)
    out = mm(y_fwd[...], stacked).astype(BF16)
    for x in range(nxb):
        sections[step * nxb + x] = out[:, x * lanes : (x + 1) * lanes]


def forward_x(sections, x_fwd, turn, out):
    pd, pp, jxl, jyl, _, lanes = out.shape
    xl = sections.shape[0]
    for p in range(pp):
        for b in range(jyl):
            j = p * jyl + b
            rows = sections[:, j * ROWS : (j + 1) * ROWS, :].reshape(xl * ROWS, lanes)
            both = jnp.concatenate([rows, mm(rows, turn[...]).astype(BF16)], 0)
            got = mm(x_fwd[...], both).astype(BF16)
            out[:, p, :, b] = got.reshape(pd, jxl, ROWS, lanes)


def inverse_x(modes, x_inv, turn, sections):
    pd, pp, jxl, jyl, _, lanes = modes.shape
    xl = sections.shape[0]
    for p in range(pp):
        for b in range(jyl):
            j = p * jyl + b
            rows = modes[:, p, :, b].reshape(pd * jxl * ROWS, lanes)
            both = jnp.concatenate([rows, mm(rows, turn[...]).astype(BF16)], 0)
            got = mm(x_inv[...], both).astype(BF16)
            sections[:, j * ROWS : (j + 1) * ROWS, :] = got.reshape(xl, ROWS, lanes)


def inverse_y(sections, turn, y_inv, columns, step, nxb):
    plain = [sections[step * nxb + x] for x in range(nxb)]
    turned = [mm(v, turn[...]).astype(BF16) for v in plain]
    stacked = jnp.concatenate([jnp.concatenate(plain, 1), jnp.concatenate(turned, 1)], 0)
    columns[...] = mm(y_inv[...], stacked).astype(BF16)


def inverse_z_mix(columns, z_inv, mix, src, emit):
    nxb, ny, ch, nz = src.shape
    groups = ch // ROWS
    lanes = z_inv.shape[0]

    def block(i, carry):
        y0 = pl.multiple_of(i * YB, YB)
        cols = columns[pl.ds(pl.multiple_of(i * (YB * ROWS), YB * ROWS), YB * ROWS), :]
        wide = jnp.concatenate([src[x, pl.ds(y0, YB)].reshape(YB * ch, nz) for x in range(nxb)], 1)
        mixed = mm(mix[...], wide)
        for x in range(nxb):
            grid = mm(cols[:, x * lanes : (x + 1) * lanes], z_inv[...]).reshape(YB, ROWS, groups * nz)
            grid = jnp.concatenate([grid[:, :, g * nz : (g + 1) * nz] for g in range(groups)], 1)
            emit(x, y0, grid + mixed[:, x * nz : (x + 1) * nz].reshape(YB, ch, nz))
        return carry

    lax.fori_loop(0, ny // YB, block, 0, unroll=2)


def gelu_slope(pre):
    normal_cdf = 0.5 * (1.0 + lax.erf(pre * (1.0 / math.sqrt(2.0))))
    return normal_cdf + pre * jnp.exp(-0.5 * pre * pre) * (1.0 / math.sqrt(2.0 * math.pi))


def first_kernel(field, z_fwd, y_fwd, x_fwd, turn, out, sections):
    step = pl.program_id(0)
    forward_zy(field, z_fwd, y_fwd, sections, step)

    @pl.when(step == pl.num_programs(0) - 1)
    def _():
        forward_x(sections, x_fwd, turn, out)


def middle_kernel(
    modes, field, target, mix, z_inv, y_inv, x_inv, z_fwd, y_fwd, x_fwd, turn,
    slope, out, sections_in, columns, sections_out,
):
    step = pl.program_id(0)

    @pl.when(step == 0)
    def _():
        inverse_x(modes, x_inv, turn, sections_in)

    inverse_y(sections_in, turn, y_inv, columns, step, field.shape[0])

    def emit(x, y0, pre):
        cot = target[x, pl.ds(y0, YB)].astype(F32)
        slope[x, pl.ds(y0, YB)] = (cot * gelu_slope(pre)).astype(BF16)

    inverse_z_mix(columns, z_inv, mix, field, emit)
    forward_zy(slope, z_fwd, y_fwd, sections_out, step)

    @pl.when(step == pl.num_programs(0) - 1)
    def _():
        forward_x(sections_out, x_fwd, turn, out)


def last_kernel(modes, slope, mix, z_adj, y_inv, x_inv, turn, grad, sections, columns):
    step = pl.program_id(0)

    @pl.when(step == 0)
    def _():
        inverse_x(modes, x_inv, turn, sections)

    inverse_y(sections, turn, y_inv, columns, step, slope.shape[0])

    def emit(x, y0, value):
        grad[x, pl.ds(y0, YB)] = value.astype(BF16)

    inverse_z_mix(columns, z_adj, mix, slope, emit)


def whole(array):
    return pl.BlockSpec(array.shape, lambda i, n=len(array.shape): (0,) * n)


def sliced(shape):
    return pl.BlockSpec((NXB,) + shape[1:], lambda i: (i, 0, 0, 0))


def params():
    return pltpu.CompilerParams(dimension_semantics=("arbitrary",), vmem_limit_bytes=VMEM)


def apply_kernel(u, w, v):
    half = u.shape[1] // 2
    ch = u.shape[2]
    for k in range(u.shape[0]):
        d = mm(u[k], w[k])
        real = d[:half, :ch] - d[half:, ch:]
        imag = d[:half, ch:] + d[half:, :ch]
        v[k] = jnp.concatenate([real, imag], 0)


def adjoint_kernel(u, g, w, grad_w, back):
    half = u.shape[1] // 2
    for k in range(u.shape[0]):
        gk = g[k]
        real, imag = gk[:half], gk[half:]
        pair = jnp.concatenate(
            [jnp.concatenate([real, imag], 1), jnp.concatenate([imag, -real], 1)], 0
        ).astype(BF16)
        back[k] = lax.dot_general(pair, w[k], (((1,), (1,)), ((), ())), preferred_element_type=F32)
        grad_w[k] = lax.dot_general(
            u[k], pair, (((0,), (0,)), ((), ())), preferred_element_type=F32
        )


def mode_call(kernel, mz, outs, *args):
    def spec(shape):
        return pl.BlockSpec((mz,) + shape[1:], lambda i: (i, 0, 0))

    return pl.pallas_call(
        kernel,
        grid=(args[0].shape[0] // mz,),
        in_specs=[spec(a.shape) for a in args],
        out_specs=[spec(o) for o in outs],
        out_shape=[jax.ShapeDtypeStruct(o, F32) for o in outs],
        compiler_params=params(),
    )(*args)


def solution(mesh):
    pd, pp = mesh.shape["dp"], mesh.shape["pencil"]
    axes = ("dp", "pencil")

    def body(field, cotangent, w_spec, w_local):
        sample, target = field[0], cotangent[0]
        xl, ny, ch, nz = sample.shape
        jxl, jyl, mz = w_spec.shape[:3]
        mx, my = jxl * pd, jyl * pp
        groups = ch // ROWS
        lanes = groups * 2 * mz
        t = make_tables(xl * pp, ny, nz, groups, mx, my, mz, pp)
        me = lax.axis_index("pencil")
        x_fwd = lax.dynamic_index_in_dim(t["x_fwd"], me, 0, keepdims=False)
        x_inv = lax.dynamic_index_in_dim(t["x_inv"], me, 0, keepdims=False)
        mix_eye = jnp.eye(YB, dtype=BF16)
        mix_in = jnp.kron(mix_eye, w_local.T)
        mix_out = jnp.kron(mix_eye, w_local)
        sent = jax.ShapeDtypeStruct((pd, pp, jxl, jyl, ROWS, lanes), BF16)
        grid_like = jax.ShapeDtypeStruct(sample.shape, BF16)
        sections = pltpu.VMEM((xl, my * ROWS, lanes), BF16)
        columns = pltpu.VMEM((ny * ROWS, NXB * lanes), BF16)
        steps = (xl // NXB,)

        def exchange(array):
            flat = array.reshape((pd * pp,) + array.shape[2:])
            return lax.all_to_all(flat, axes, split_axis=0, concat_axis=0, tiled=True)

        def gather_modes(parts):
            got = exchange(parts).reshape((pd, pp, jxl, jyl, ROWS, lanes))
            return got.astype(F32).sum(1)

        def per_mode(total):
            split = total.reshape(pd, jxl, jyl, ROWS, groups, 2, mz)
            turned = split.transpose(1, 2, 6, 5, 0, 4, 3)
            return turned.reshape(jxl * jyl * mz, 2 * pd, ch)

        def to_samples(modes):
            split = modes.astype(BF16).reshape(jxl, jyl, mz, 2, pd, groups, ROWS)
            turned = split.transpose(4, 0, 1, 6, 5, 3, 2).reshape(pd, 1, jxl, jyl, ROWS, lanes)
            out = jnp.broadcast_to(turned, (pd, pp) + turned.shape[2:])
            return exchange(out).reshape(sent.shape)

        weights = w_spec.reshape(jxl * jyl * mz, ch, 2 * ch)
        ins = (sample, t["z_fwd"], t["y_fwd"], x_fwd, t["turn"])
        u_parts = pl.pallas_call(
            first_kernel,
            grid=steps,
            in_specs=[sliced(sample.shape)] + [whole(a) for a in ins[1:]],
            out_specs=whole(sent),
            out_shape=sent,
            scratch_shapes=[sections],
            compiler_params=params(),
        )(*ins)
        u_modes = per_mode(gather_modes(u_parts)).astype(BF16)
        (v_modes,) = mode_call(apply_kernel, mz, [u_modes.shape], u_modes, weights)
        ins = (
            to_samples(v_modes), sample, target, mix_in, t["z_inv"], t["y_inv"], x_inv,
            t["z_fwd"], t["y_fwd"], x_fwd, t["turn"],
        )
        slope, g_parts = pl.pallas_call(
            middle_kernel,
            grid=steps,
            in_specs=[whole(ins[0]), sliced(sample.shape), sliced(sample.shape)]
            + [whole(a) for a in ins[3:]],
            out_specs=[sliced(sample.shape), whole(sent)],
            out_shape=[grid_like, sent],
            scratch_shapes=[sections, columns, sections],
            compiler_params=params(),
        )(*ins)
        g_modes = per_mode(gather_modes(g_parts) * t["scale"]).astype(BF16).astype(F32)
        grad_w, back = mode_call(
            adjoint_kernel, mz, [weights.shape, u_modes.shape], u_modes, g_modes, weights
        )
        ins = (to_samples(back), slope, mix_out, t["z_adj"], t["y_inv"], x_inv, t["turn"])
        grad = pl.pallas_call(
            last_kernel,
            grid=steps,
            in_specs=[whole(ins[0]), sliced(sample.shape)] + [whole(a) for a in ins[2:]],
            out_specs=sliced(sample.shape),
            out_shape=grid_like,
            scratch_shapes=[sections, columns],
            compiler_params=params(),
        )(*ins)
        return grad[None], grad_w.reshape(w_spec.shape)

    grid_spec = P("dp", "pencil", None, None, None)
    return jax.shard_map(
        body,
        mesh=mesh,
        in_specs=(grid_spec, grid_spec, grid_spec, P()),
        out_specs=(grid_spec, grid_spec),
        check_vma=False,
    )
```

time: 630 us -> 309 us (0.49)
  matrix products: 370 us -> 0 us
  Pallas kernels: 0 us -> 115 us
  other arithmetic: 38.9 us -> 10.4 us
  waiting for transfers between devices: 70.6 us -> 48.9 us
  blocking collectives: 69.3 us -> 62.9 us
    dot_general x28 -> x0, matrix products: 370 us -> none  [the longest x2 130 us: z_back(): jnp.dot(values.reshape(-1, shape_in[-1]), matrix, precision=HIGHEST, pref...]
    pallas_call x0 -> x5, Pallas kernels: none -> 115 us  [the longest x1 52.9 us: body(): pl.pallas_call(middle_kernel, grid=steps, in_specs=[whole(ins[0]), sliced...]
    unnamed x41 -> x8, local copies, waits for them, and re-layouts: 32 us -> 1.96 us
    slice x8 -> x0, other arithmetic: 22.5 us -> none  [rotate_half(): return jnp.concatenate([values[..., middle:], -values[..., :middle]], -1)]
    all_to_all x3 -> x2, waiting for transfers between devices: 70.6 us -> 48.9 us  [exchange(): return lax.all_to_all(flat, axes, split_axis=0, concat_axis=0, tiled=True)]
    convert_element_type x4 -> x7, local copies, waits for them, and re-layouts: 9.07 us -> 24.1 us  [the longest x2 12.5 us: body(): per_mode(gather_modes(g_parts) * t['scale']).astype(BF16).astype(F32)]
    broadcast_in_dim x2 -> x4, local copies, waits for them, and re-layouts: 0.27 us -> 15.3 us  [to_samples(): out = jnp.broadcast_to(turned, (pd, pp) + turned.shape[2:])]
    concatenate x4 -> x0, other arithmetic: 12.3 us -> none  [the longest x1 12 us: rotate_half(): return jnp.concatenate([values[..., middle:], -values[..., :middle]], -1)]
  transfers between devices with their start and end apart: 3 -> 2, of which waited for: 3 -> 2; matrix products, arithmetic and copies ran while one was open for 1% -> 1% of each run, Pallas kernels for 0% -> 0%
where the time goes in v1:
time: 309 us; the launch traced here: 307 us
  Pallas kernels  115 us (37%)
  local copies, waits for them, and re-layouts  63 us (20%)
  blocking collectives  62.9 us (20%)
  waiting for transfers between devices  48.9 us (16%)
  other arithmetic  10.4 us (3%)
  starting transfers between devices  6.32 us (2%)
    all_to_all x2, blocking collectives, exchange(): return lax.all_to_all(flat, axes, split_axis=0, concat_axis=0, tiled=True)  62.9 us
    pallas_call x1, Pallas kernels, body(): pl.pallas_call(middle_kernel, grid=steps, in_specs=[whole(ins[0]), sliced...  52.9 us
    all_to_all x2, waiting for transfers between devices, exchange(): return lax.all_to_all(flat, axes, split_axis=0, concat_axis=0, tiled=True)  48.9 us
    pallas_call x1, Pallas kernels, body(): pl.pallas_call(last_kernel, grid=steps, in_specs=[whole(ins[0]), sliced(s...  29.7 us
    pallas_call x1, Pallas kernels, body(): pl.pallas_call(first_kernel, grid=steps, in_specs=[sliced(sample.shape)]...  17.5 us
    broadcast_in_dim x4, local copies, waits for them, and re-layouts, to_samples(): out = jnp.broadcast_to(turned, (pd, pp) + turned.shape[2:])  15.3 us
    pallas_call x2, Pallas kernels, mode_call(): pl.pallas_call(kernel, grid=(args[0].shape[0] // mz,), in_specs=[spec(a.s...  14.7 us
    convert_element_type x2, local copies, waits for them, and re-layouts, body(): per_mode(gather_modes(g_parts) * t['scale']).astype(BF16).astype(F32)  12.5 us
  transfers between devices with their start and end apart: 2, of which 2 were waited for; matrix products, arithmetic and copies ran while one was open for 1% of the time, Pallas kernels for 0%

profile of v1, /device:TPU:1, one launch (start us, length us, event | category | flops | bytes accessed | tf_op | source)
XLA Modules:
  0.0 307.0 jit_solution(17319086113833772861)
XLA Ops:
  0.6 1.7 dynamic-slice_bitcast_fusion.1.x_fwd
  2.3 17.5 %shard_map.140 = bf16[8,4,2,4,16,128]{5,4,3,2,1,0:T(8,128)(2,1)} custom-call(bf16[16,64,64,128]{3,2,1,0:T(8,128)(2,1)} %bitcast.34, bf16[512,256]{1,0:T(8,128)(2,1)} %constant.32.clone.z_fwd, bf16[256,2048]{1,0:T(8,128)(2,1)} %constant.36.clone.y_fwd, bf16[256,512]{1,0:T(8,128)(2,1)} %dynamic-slice_bitcast_fusion.1.x_fwd, bf16[128,128]{1,0:T(8,128)(2,1)} %constant.35.clone.turn), custom_call_target="tpu_custom_call" | custom-call | tf_op jit(solution)/shard_map/pallas_call | solution.py:291
  19.8 33.4 %all_to_all.20 = bf16[32,2,4,16,128]{4,3,2,1,0:T(8,128)(2,1)S(1)} all-to-all(bf16[32,2,4,16,128]{4,3,2,1,0:T(8,128)(2,1)} %bitcast.45), channel_id=1, replica_groups=mesh['dp'=8,'pencil'=4] {'dp','pencil'}, dimensions={0} | all-to-all | bytes 2097152 | tf_op jit(solution)/shard_map/all_to_all | solution.py:272
  53.2 0.2 bitcast_reduce_fusion
  53.4 2.3 convert_element_type.51
  55.8 6.6 %copy.36 = bf16[2,4,16,2,8,4,16]{6,5,4,3,2,1,0:T(4,128)(2,1)S(1)} copy(bf16[2,4,16,2,8,4,16]{2,3,5,6,1,0,4:T(2,128)(2,1)} %bitcast.40) | data formatting | bytes 524288 | tf_op jit(solution)/shard_map/convert_element_type | solution.py:300
  62.4 1.8 reshape.88.u
  64.1 6.7 %shard_map.141 = f32[128,16,64]{2,1,0:T(8,128)} custom-call(bf16[128,16,64]{2,1,0:T(8,128)(2,1)} %reshape.88.u, bf16[128,64,128]{2,1,0:T(8,128)(2,1)} %bitcast.38), custom_call_target="tpu_custom_call" | custom-call | tf_op jit(solution)/shard_map/pallas_call | solution.py:236
  70.9 1.3 convert_element_type.54
  72.2 0.5 copy.28
  72.6 1.4 reshape.78
  74.0 0.0 copy-start.2
  74.0 3.5 %copy.29 = bf16[8,2,4,16,4,2,16]{6,5,4,3,2,1,0:T(2,128)(2,1)} copy(bf16[8,2,4,16,4,2,16]{6,2,1,3,4,0,5:T(4,128)(2,1)S(1)} %bitcast.41) | data formatting | bytes 524288 | tf_op jit(solution)/shard_map/transpose | solution.py:285
  77.5 6.4 %broadcast_in_dim.24 = bf16[8,2,4,16,128]{4,3,2,1,0:T(8,128)(2,1)S(1)} reshape(bf16[8,2,4,16,4,2,16]{6,5,4,3,2,1,0:T(2,128)(2,1)} %copy.29) | data formatting | bytes 524288 | tf_op jit(solution)/shard_map/broadcast_in_dim | solution.py:286
  84.0 1.2 broadcast_in_dim.25
  85.2 3.2 %all-to-all-start.1 = ((bf16[32,2,4,16,128]{4,3,2,1,0:T(8,128)(2,1)}), bf16[32,2,4,16,128]{4,3,2,1,0:T(8,128)(2,1)S(1)}, u32[]{:S(2)}, u32[]{:S(2)}) async-start(bf16[32,2,4,16,128]{4,3,2,1,0:T(8,128)(2,1)} %bitcast.7), calls=%async_computation.1 | async-start | bytes 2097152 | tf_op jit(solution)/shard_map/all_to_all | solution.py:272
  88.4 0.0 copy-done.2
  88.4 0.1 copy.30
  88.5 0.3 broadcast_multiply_fusion
  88.7 0.9 mul.55.mix
  89.6 1.7 dynamic-slice_bitcast_fusion.x_inv
  91.3 23.4 %all-to-all-done.1 = bf16[32,2,4,16,128]{4,3,2,1,0:T(8,128)(2,1)S(1)} async-done(((bf16[32,2,4,16,128]{4,3,2,1,0:T(8,128)(2,1)}), bf16[32,2,4,16,128]{4,3,2,1,0:T(8,128)(2,1)S(1)}, u32[]{:S(2)}, u32[]{:S(2)}) %all-to-all-start.1) | async-done | bytes 1048608 | tf_op jit(solution)/shard_map/all_to_all | solution.py:272
  114.7 0.0 copy-start
  114.7 1.0 copy-done
  115.7 52.9 %shard_map.142 = (bf16[16,64,64,128]{3,2,1,0:T(8,128)(2,1)}, bf16[8,4,2,4,16,128]{5,4,3,2,1,0:T(8,128)(2,1)}) custom-call(bf16[8,4,2,4,16,128]{5,4,3,2,1,0:T(8,128)(2,1)} %bitcast.43, bf16[16,64,64,128]{3,2,1,0:T(8,128)(2,1)} %bitcast.35, bf16[16,64,64,128]{3,2,1,0:T(8,128)(2,1)} %bitcast.37, bf16[256,256]{1,0:T(8,128)(2,1)} %mul.55.mix, ...), custom_call_target="tpu_custom_call" | custom-call | tf_op jit(solution)/shard_map/pallas_call | solution.py:306
  168.6 0.0 copy-start.3
  168.6 29.5 %all_to_all.21 = bf16[32,2,4,16,128]{4,3,2,1,0:T(8,128)(2,1)S(1)} all-to-all(bf16[32,2,4,16,128]{4,3,2,1,0:T(8,128)(2,1)} %bitcast.46), channel_id=1, replica_groups=mesh['dp'=8,'pencil'=4] {'dp','pencil'}, dimensions={0} | all-to-all | bytes 2097152 | tf_op jit(solution)/shard_map/all_to_all | solution.py:272
  198.1 0.2 convert_reduce_fusion
  198.3 6.7 %reduce_sum.22 = f32[8,2,4,16,4,2,16]{6,5,4,3,2,1,0:T(2,128)} reshape(f32[8,2,4,16,128]{4,3,2,1,0:T(8,128)S(1)} %convert_reduce_fusion) | data formatting | bytes 1048576 | tf_op jit(solution)/shard_map/reduce_sum | solution.py:276
  205.0 0.0 copy-done.3
  205.0 7.1 %convert_bitcast_fusion = f32[2,4,16,2,8,4,16]{2,3,5,6,1,0,4:T(2,128)} fusion(f32[8,2,4,16,4,2,16]{6,5,4,3,2,1,0:T(2,128)} %reduce_sum.22, f32[4,2,16]{2,1,0:T(2,128)S(1)} %copy-done.3), kind=kLoop, calls=%fused_computation | loop fusion | flops 393216 | bytes 1049088 | tf_op jit(solution)/shard_map/convert_element_type | solution.py:316
  212.2 8.0 %copy.38 = f32[2,4,16,2,8,4,16]{6,5,4,3,2,1,0:T(4,128)} copy(f32[2,4,16,2,8,4,16]{2,3,5,6,1,0,4:T(2,128)} %convert_bitcast_fusion) | data formatting | bytes 1048576 | tf_op jit(solution)/shard_map/convert_element_type | solution.py:316
  220.1 4.5 %reshape.89.g = f32[128,16,64]{2,1,0:T(8,128)} reshape(f32[2,4,16,2,8,4,16]{6,5,4,3,2,1,0:T(4,128)} %copy.38) | data formatting | bytes 1048576 | tf_op jit(solution)/shard_map/convert_element_type | solution.py:316
  224.7 7.9 %shard_map.143 = (f32[128,64,128]{2,1,0:T(8,128)}, f32[128,16,64]{2,1,0:T(8,128)}) custom-call(bf16[128,16,64]{2,1,0:T(8,128)(2,1)} %reshape.88.u, f32[128,16,64]{2,1,0:T(8,128)} %reshape.89.g, bf16[128,64,128]{2,1,0:T(8,128)(2,1)} %bitcast.39), custom_call_target="tpu_custom_call" | custom-call | tf_op jit(solution)/shard_map/pallas_call | solution.py:236
  232.6 1.3 convert_element_type.62
  233.9 0.5 copy.34
  234.4 1.4 reshape.82
  235.8 3.5 %copy.35 = bf16[8,2,4,16,4,2,16]{6,5,4,3,2,1,0:T(2,128)(2,1)} copy(bf16[8,2,4,16,4,2,16]{6,2,1,3,4,0,5:T(4,128)(2,1)S(1)} %bitcast.42) | data formatting | bytes 524288 | tf_op jit(solution)/shard_map/transpose | solution.py:285
  239.3 6.4 %broadcast_in_dim.26 = bf16[8,2,4,16,128]{4,3,2,1,0:T(8,128)(2,1)S(1)} reshape(bf16[8,2,4,16,4,2,16]{6,5,4,3,2,1,0:T(2,128)(2,1)} %copy.35) | data formatting | bytes 524288 | tf_op jit(solution)/shard_map/broadcast_in_dim | solution.py:286
  245.7 1.2 broadcast_in_dim.27
  246.9 3.2 %all-to-all-start.3 = ((bf16[32,2,4,16,128]{4,3,2,1,0:T(8,128)(2,1)}), bf16[32,2,4,16,128]{4,3,2,1,0:T(8,128)(2,1)S(1)}, u32[]{:S(2)}, u32[]{:S(2)}) async-start(bf16[32,2,4,16,128]{4,3,2,1,0:T(8,128)(2,1)} %bitcast.16), calls=%async_computation.3 | async-start | bytes 2097152 | tf_op jit(solution)/shard_map/all_to_all | solution.py:272
  250.1 0.9 mul.61.mix
  250.9 25.5 %all-to-all-done.3 = bf16[32,2,4,16,128]{4,3,2,1,0:T(8,128)(2,1)S(1)} async-done(((bf16[32,2,4,16,128]{4,3,2,1,0:T(8,128)(2,1)}), bf16[32,2,4,16,128]{4,3,2,1,0:T(8,128)(2,1)S(1)}, u32[]{:S(2)}, u32[]{:S(2)}) %all-to-all-start.3) | async-done | bytes 1048608 | tf_op jit(solution)/shard_map/all_to_all | solution.py:272
  276.4 0.0 copy-start.1
  276.4 1.0 copy-done.1
  277.4 29.7 %shard_map.144 = bf16[16,64,64,128]{3,2,1,0:T(8,128)(2,1)} custom-call(bf16[8,4,2,4,16,128]{5,4,3,2,1,0:T(8,128)(2,1)} %bitcast.44, bf16[16,64,64,128]{3,2,1,0:T(8,128)(2,1)} %get-tuple-element.8.slope, bf16[256,256]{1,0:T(8,128)(2,1)} %mul.61.mix, bf16[128,512]{1,0:T(8,128)(2,1)} %constant.34.clone.z_adj, bf16[1024,512]{1,0:T(8,128)(2,1)} %constant.37.clone.y_inv, ...), custom_call_target="tpu_custom_call" | custom-call | tf_op jit(solution)/shard_map/pallas_call | solution.py:321
  (1 shorter events, 0.0 us)
Async XLA Ops:
  74.0 14.3 %copy-start.2 = (bf16[64,64]{1,0:T(8,128)(2,1)S(1)}, bf16[64,64]{1,0:T(8,128)(2,1)}, u32[]{:S(2)}) copy-start(bf16[64,64]{1,0:T(8,128)(2,1)} %param.16) | copy-start | bytes 24580
  85.2 29.5 %all-to-all-start.1 = ((bf16[32,2,4,16,128]{4,3,2,1,0:T(8,128)(2,1)}), bf16[32,2,4,16,128]{4,3,2,1,0:T(8,128)(2,1)S(1)}, u32[]{:S(2)}, u32[]{:S(2)}) async-start(bf16[32,2,4,16,128]{4,3,2,1,0:T(8,128)(2,1)} %bitcast.7), calls=%async_computation.1 | async-start | bytes 2097152 | tf_op jit(solution)/shard_map/all_to_all | solution.py:272
  114.7 1.0 copy-start
  168.6 36.4 %copy-start.3 = (f32[4,2,16]{2,1,0:T(2,128)S(1)}, f32[4,2,16]{2,1,0:T(2,128)}, u32[]{:S(2)}) copy-start(f32[4,2,16]{2,1,0:T(2,128)} %constant.44) | copy-start | bytes 1540
  246.9 29.5 %all-to-all-start.3 = ((bf16[32,2,4,16,128]{4,3,2,1,0:T(8,128)(2,1)}), bf16[32,2,4,16,128]{4,3,2,1,0:T(8,128)(2,1)S(1)}, u32[]{:S(2)}, u32[]{:S(2)}) async-start(bf16[32,2,4,16,128]{4,3,2,1,0:T(8,128)(2,1)} %bitcast.16), calls=%async_computation.3 | async-start | bytes 2097152 | tf_op jit(solution)/shard_map/all_to_all | solution.py:272
  276.4 1.0 copy-start.1

commit v2 on v1

--- a/solution.py
+++ b/solution.py
@@ -205,42 +205,83 @@
     return pltpu.CompilerParams(dimension_semantics=("arbitrary",), vmem_limit_bytes=VMEM)
 
 
-def apply_kernel(u, w, v):
-    half = u.shape[1] // 2
-    ch = u.shape[2]
-    for k in range(u.shape[0]):
-        d = mm(u[k], w[k])
-        real = d[:half, :ch] - d[half:, ch:]
-        imag = d[:half, ch:] + d[half:, :ch]
-        v[k] = jnp.concatenate([real, imag], 0)
-
-
-def adjoint_kernel(u, g, w, grad_w, back):
-    half = u.shape[1] // 2
-    for k in range(u.shape[0]):
-        gk = g[k]
-        real, imag = gk[:half], gk[half:]
+def load_modes(parts, scale, by_mode):
+    pd, pp, _, rows, lanes = parts.shape
+    total = parts[:, 0, 0].astype(F32)
+    for q in range(1, pp):
+        total = total + parts[:, q, 0].astype(F32)
+    total = total * scale[...]
+    turned = total.reshape(pd * rows, lanes).T
+    count = by_mode.shape[0]
+    for s in range(pd):
+        own = turned[:, s * rows : (s + 1) * rows]
+        pieces = [own[g * count : (g + 1) * count] for g in range(lanes // count)]
+        by_mode[:, s, :] = jnp.concatenate(pieces, 1)
+
+
+def store_modes(by_mode, out):
+    pd, pp, _, rows, lanes = out.shape
+    count = by_mode.shape[0]
+    columns = []
+    for s in range(pd):
+        own = by_mode[:, s, :]
+        pieces = [own[:, g * rows : (g + 1) * rows] for g in range(lanes // count)]
+        columns.append(jnp.concatenate(pieces, 0))
+    turned = jnp.concatenate(columns, 1).T.reshape(pd, rows, lanes).astype(BF16)
+    for q in range(pp):
+        out[:, q, 0] = turned
+
+
+def apply_kernel(parts, w, scale, u, out, by_mode, result):
+    load_modes(parts, scale, by_mode)
+    mz, ch = w.shape[0], w.shape[1]
+    half = by_mode.shape[1]
+    for k in range(mz):
+        uk = jnp.concatenate([by_mode[k], by_mode[mz + k]], 0).astype(BF16)
+        u[k] = uk
+        d = mm(uk, w[k])
+        result[k] = d[:half, :ch] - d[half:, ch:]
+        result[mz + k] = d[:half, ch:] + d[half:, :ch]
+    store_modes(result, out)
+
+
+def adjoint_kernel(parts, w, scale, u, grad_w, out, by_mode, result):
+    load_modes(parts, scale, by_mode)
+    mz = w.shape[0]
+    half = by_mode.shape[1]
+    for k in range(mz):
+        real, imag = by_mode[k], by_mode[mz + k]
         pair = jnp.concatenate(
             [jnp.concatenate([real, imag], 1), jnp.concatenate([imag, -real], 1)], 0
         ).astype(BF16)
-        back[k] = lax.dot_general(pair, w[k], (((1,), (1,)), ((), ())), preferred_element_type=F32)
+        back = lax.dot_general(pair, w[k], (((1,), (1,)), ((), ())), preferred_element_type=F32)
+        result[k] = back[:half]
+        result[mz + k] = back[half:]
         grad_w[k] = lax.dot_general(
             u[k], pair, (((0,), (0,)), ((), ())), preferred_element_type=F32
         )
-
-
-def mode_call(kernel, mz, outs, *args):
-    def spec(shape):
-        return pl.BlockSpec((mz,) + shape[1:], lambda i: (i, 0, 0))
-
+    store_modes(result, out)
+
+
+def mode_call(kernel, parts, w, scale, u):
+    pd, pp, count, rows, lanes = parts.shape
+    mz, ch = w.shape[0] // count, w.shape[1]
+    first = u is None
+    part_spec = pl.BlockSpec((pd, pp, 1, rows, lanes), lambda i: (0, 0, i, 0, 0))
+    w_spec = pl.BlockSpec((mz,) + w.shape[1:], lambda i: (i, 0, 0))
+    u_spec = pl.BlockSpec((mz, 2 * pd, ch), lambda i: (i, 0, 0))
+    u_shape = jax.ShapeDtypeStruct((w.shape[0], 2 * pd, ch), BF16)
+    w_shape = jax.ShapeDtypeStruct(w.shape, F32)
+    by_mode = pltpu.VMEM((2 * mz, pd, ch), F32)
     return pl.pallas_call(
         kernel,
-        grid=(args[0].shape[0] // mz,),
-        in_specs=[spec(a.shape) for a in args],
-        out_specs=[spec(o) for o in outs],
-        out_shape=[jax.ShapeDtypeStruct(o, F32) for o in outs],
+        grid=(count,),
+        in_specs=[part_spec, w_spec, whole(scale)] + ([] if first else [u_spec]),
+        out_specs=[u_spec if first else w_spec, part_spec],
+        out_shape=[u_shape if first else w_shape, jax.ShapeDtypeStruct(parts.shape, BF16)],
+        scratch_shapes=[by_mode, by_mode],
         compiler_params=params(),
-    )(*args)
+    )(parts, w, scale, *(() if first else (u,)))
 
 
 def solution(mesh):
@@ -269,22 +310,14 @@
 
         def exchange(array):
             flat = array.reshape((pd * pp,) + array.shape[2:])
-            return lax.all_to_all(flat, axes, split_axis=0, concat_axis=0, tiled=True)
-
-        def gather_modes(parts):
-            got = exchange(parts).reshape((pd, pp, jxl, jyl, ROWS, lanes))
-            return got.astype(F32).sum(1)
-
-        def per_mode(total):
-            split = total.reshape(pd, jxl, jyl, ROWS, groups, 2, mz)
-            turned = split.transpose(1, 2, 6, 5, 0, 4, 3)
-            return turned.reshape(jxl * jyl * mz, 2 * pd, ch)
-
-        def to_samples(modes):
-            split = modes.astype(BF16).reshape(jxl, jyl, mz, 2, pd, groups, ROWS)
-            turned = split.transpose(4, 0, 1, 6, 5, 3, 2).reshape(pd, 1, jxl, jyl, ROWS, lanes)
-            out = jnp.broadcast_to(turned, (pd, pp) + turned.shape[2:])
-            return exchange(out).reshape(sent.shape)
+            got = lax.all_to_all(flat, axes, split_axis=0, concat_axis=0, tiled=True)
+            return got.reshape(array.shape)
+
+        def to_owner(parts):
+            return exchange(parts).reshape((pd, pp, jxl * jyl, ROWS, lanes))
+
+        def to_sample(modes):
+            return exchange(modes).reshape(sent.shape)
 
         weights = w_spec.reshape(jxl * jyl * mz, ch, 2 * ch)
         ins = (sample, t["z_fwd"], t["y_fwd"], x_fwd, t["turn"])
@@ -297,10 +330,12 @@
             scratch_shapes=[sections],
             compiler_params=params(),
         )(*ins)
-        u_modes = per_mode(gather_modes(u_parts)).astype(BF16)
-        (v_modes,) = mode_call(apply_kernel, mz, [u_modes.shape], u_modes, weights)
+        scale = t["scale"].reshape(1, 1, lanes)
+        u_modes, v_modes = mode_call(
+            apply_kernel, to_owner(u_parts), weights, jnp.ones_like(scale), None
+        )
         ins = (
-            to_samples(v_modes), sample, target, mix_in, t["z_inv"], t["y_inv"], x_inv,
+            to_sample(v_modes), sample, target, mix_in, t["z_inv"], t["y_inv"], x_inv,
             t["z_fwd"], t["y_fwd"], x_fwd, t["turn"],
         )
         slope, g_parts = pl.pallas_call(
@@ -313,11 +348,8 @@
             scratch_shapes=[sections, columns, sections],
             compiler_params=params(),
         )(*ins)
-        g_modes = per_mode(gather_modes(g_parts) * t["scale"]).astype(BF16).astype(F32)
-        grad_w, back = mode_call(
-            adjoint_kernel, mz, [weights.shape, u_modes.shape], u_modes, g_modes, weights
-        )
-        ins = (to_samples(back), slope, mix_out, t["z_adj"], t["y_inv"], x_inv, t["turn"])
+        grad_w, back = mode_call(adjoint_kernel, to_owner(g_parts), weights, scale, u_modes)
+        ins = (to_sample(back), slope, mix_out, t["z_adj"], t["y_inv"], x_inv, t["turn"])
         grad = pl.pallas_call(
             last_kernel,
             grid=steps,

time: 309 us -> 247 us (0.80)
  local copies, waits for them, and re-layouts: 63 us -> 7.66 us
  other arithmetic: 10.4 us -> 0.27 us
  Pallas kernels: 115 us -> 119 us
    convert_element_type x7 -> x0, local copies, waits for them, and re-layouts: 24.1 us -> none  [the longest x2 12.5 us: body(): per_mode(gather_modes(g_parts) * t['scale']).astype(BF16).astype(F32)]
    broadcast_in_dim x4 -> x1, local copies, waits for them, and re-layouts: 15.3 us -> 0.51 us  [body(): jnp.ones_like(scale)]
    convert_element_type x3 -> x0, other arithmetic: 9.72 us -> none  [the longest x1 7.13 us: body(): per_mode(gather_modes(g_parts) * t['scale']).astype(BF16).astype(F32)]
    transpose x2 -> x0, local copies, waits for them, and re-layouts: 7.03 us -> none  [to_samples(): split.transpose(4, 0, 1, 6, 5, 3, 2).reshape(pd, 1, jxl, jyl, ROWS, lanes)]
    reduce_sum x1 -> x0, local copies, waits for them, and re-layouts: 6.72 us -> none  [gather_modes(): return got.astype(F32).sum(1)]
    pallas_call x2, Pallas kernels: 14.7 us -> 19.3 us  [mode_call(): pl.pallas_call(kernel, grid=(count,), in_specs=[part_spec, w_spec, whole(...]
  transfers between devices with their start and end apart: 2 -> 2, of which waited for: 2 -> 2; matrix products, arithmetic and copies ran while one was open for 1% -> 2% of each run, Pallas kernels for 0% -> 0%
where the time goes in v2:
time: 247 us; the launch traced here: 246 us
  Pallas kernels  119 us (48%)
  blocking collectives  63.1 us (26%)
  waiting for transfers between devices  48.8 us (20%)
  local copies, waits for them, and re-layouts  7.66 us (3%)
  starting transfers between devices  6.31 us (3%)
    all_to_all x2, blocking collectives, exchange(): got = lax.all_to_all(flat, axes, split_axis=0, concat_axis=0, tiled=True)  63.1 us
    pallas_call x1, Pallas kernels, body(): pl.pallas_call(middle_kernel, grid=steps, in_specs=[whole(ins[0]), sliced...  52.9 us
    all_to_all x2, waiting for transfers between devices, exchange(): got = lax.all_to_all(flat, axes, split_axis=0, concat_axis=0, tiled=True)  48.8 us
    pallas_call x1, Pallas kernels, body(): pl.pallas_call(last_kernel, grid=steps, in_specs=[whole(ins[0]), sliced(s...  29.7 us
    pallas_call x2, Pallas kernels, mode_call(): pl.pallas_call(kernel, grid=(count,), in_specs=[part_spec, w_spec, whole(...  19.3 us
    pallas_call x1, Pallas kernels, body(): pl.pallas_call(first_kernel, grid=steps, in_specs=[sliced(sample.shape)]...  17.5 us
    all_to_all x2, starting transfers between devices, exchange(): got = lax.all_to_all(flat, axes, split_axis=0, concat_axis=0, tiled=True)  6.31 us
  transfers between devices with their start and end apart: 2, of which 2 were waited for; matrix products, arithmetic and copies ran while one was open for 2% of the time, Pallas kernels for 0%

profile of v2, /device:TPU:1, one launch (start us, length us, event | category | flops | bytes accessed | tf_op | source)
XLA Modules:
  0.0 246.3 jit_solution(13620893927349603949)
XLA Ops:
  0.6 0.0 copy-start.2
  0.6 1.7 dynamic-slice_bitcast_fusion.1.x_fwd
  2.3 17.5 %shard_map.140 = bf16[8,4,2,4,16,128]{5,4,3,2,1,0:T(8,128)(2,1)} custom-call(bf16[16,64,64,128]{3,2,1,0:T(8,128)(2,1)} %bitcast.18, bf16[512,256]{1,0:T(8,128)(2,1)} %constant.32.clone.z_fwd, bf16[256,2048]{1,0:T(8,128)(2,1)} %constant.36.clone.y_fwd, bf16[256,512]{1,0:T(8,128)(2,1)} %dynamic-slice_bitcast_fusion.1.x_fwd, bf16[128,128]{1,0:T(8,128)(2,1)} %constant.35.clone.turn), custom_call_target="tpu_custom_call" | custom-call | tf_op jit(solution)/shard_map/pallas_call | solution.py:324
  19.8 33.5 %all_to_all.20 = bf16[32,2,4,16,128]{4,3,2,1,0:T(8,128)(2,1)} all-to-all(bf16[32,2,4,16,128]{4,3,2,1,0:T(8,128)(2,1)} %bitcast.26), channel_id=1, replica_groups=mesh['dp'=8,'pencil'=4] {'dp','pencil'}, dimensions={0} | all-to-all | bytes 2097152 | tf_op jit(solution)/shard_map/all_to_all | solution.py:313
  53.4 0.5 broadcast_in_dim.12.scale
  53.9 9.5 %shard_map.141 = (bf16[128,16,64]{2,1,0:T(8,128)(2,1)}, bf16[8,4,8,16,128]{4,3,2,1,0:T(8,128)(2,1)}) custom-call(bf16[8,4,8,16,128]{4,3,2,1,0:T(8,128)(2,1)} %bitcast.27, bf16[128,64,128]{2,1,0:T(8,128)(2,1)} %bitcast.22, f32[1,1,128]{2,1,0:T(1,128)} %broadcast_in_dim.12.scale), custom_call_target="tpu_custom_call" | custom-call | tf_op jit(solution)/shard_map/pallas_call | solution.py:276
  63.4 3.2 %all-to-all-start.1 = ((bf16[32,8,16,128]{3,2,1,0:T(8,128)(2,1)}), bf16[32,8,16,128]{3,2,1,0:T(8,128)(2,1)S(1)}, u32[]{:S(2)}, u32[]{:S(2)}) async-start(bf16[32,8,16,128]{3,2,1,0:T(8,128)(2,1)} %bitcast.29), calls=%async_computation.1 | async-start | bytes 2097152 | tf_op jit(solution)/shard_map/all_to_all | solution.py:313
  66.5 0.0 copy-done.2
  66.6 0.1 copy.15
  66.7 0.3 broadcast_multiply_fusion
  66.9 0.9 mul.44.mix
  67.8 1.7 dynamic-slice_bitcast_fusion.x_inv
  69.5 23.4 %all-to-all-done.1 = bf16[32,8,16,128]{3,2,1,0:T(8,128)(2,1)S(1)} async-done(((bf16[32,8,16,128]{3,2,1,0:T(8,128)(2,1)}), bf16[32,8,16,128]{3,2,1,0:T(8,128)(2,1)S(1)}, u32[]{:S(2)}, u32[]{:S(2)}) %all-to-all-start.1) | async-done | bytes 1048608 | tf_op jit(solution)/shard_map/all_to_all | solution.py:313
  92.9 0.0 copy-start
  92.9 1.0 copy-done
  93.8 52.9 %shard_map.142 = (bf16[16,64,64,128]{3,2,1,0:T(8,128)(2,1)}, bf16[8,4,2,4,16,128]{5,4,3,2,1,0:T(8,128)(2,1)}) custom-call(bf16[8,4,2,4,16,128]{5,4,3,2,1,0:T(8,128)(2,1)} %bitcast.24, bf16[16,64,64,128]{3,2,1,0:T(8,128)(2,1)} %bitcast.19, bf16[16,64,64,128]{3,2,1,0:T(8,128)(2,1)} %bitcast.21, bf16[256,256]{1,0:T(8,128)(2,1)} %mul.44.mix, ...), custom_call_target="tpu_custom_call" | custom-call | tf_op jit(solution)/shard_map/pallas_call | solution.py:341
  146.8 29.6 %all_to_all.21 = bf16[32,2,4,16,128]{4,3,2,1,0:T(8,128)(2,1)} all-to-all(bf16[32,2,4,16,128]{4,3,2,1,0:T(8,128)(2,1)} %bitcast.31), channel_id=1, replica_groups=mesh['dp'=8,'pencil'=4] {'dp','pencil'}, dimensions={0} | all-to-all | bytes 2097152 | tf_op jit(solution)/shard_map/all_to_all | solution.py:313
  176.4 9.8 %shard_map.143 = (f32[128,64,128]{2,1,0:T(8,128)}, bf16[8,4,8,16,128]{4,3,2,1,0:T(8,128)(2,1)}) custom-call(bf16[8,4,8,16,128]{4,3,2,1,0:T(8,128)(2,1)} %bitcast.28, bf16[128,64,128]{2,1,0:T(8,128)(2,1)} %bitcast.23, f32[1,1,128]{2,1,0:T(1,128)} %constant.44.scale, bf16[128,16,64]{2,1,0:T(8,128)(2,1)} %get-tuple-element.10.u), custom_call_target="tpu_custom_call" | custom-call | tf_op jit(solution)/shard_map/pallas_call | solution.py:276
  186.2 3.2 %all-to-all-start.3 = ((bf16[32,8,16,128]{3,2,1,0:T(8,128)(2,1)}), bf16[32,8,16,128]{3,2,1,0:T(8,128)(2,1)S(1)}, u32[]{:S(2)}, u32[]{:S(2)}) async-start(bf16[32,8,16,128]{3,2,1,0:T(8,128)(2,1)} %bitcast.30), calls=%async_computation.3 | async-start | bytes 2097152 | tf_op jit(solution)/shard_map/all_to_all | solution.py:313
  189.4 0.9 mul.47.mix
  190.3 25.4 %all-to-all-done.3 = bf16[32,8,16,128]{3,2,1,0:T(8,128)(2,1)S(1)} async-done(((bf16[32,8,16,128]{3,2,1,0:T(8,128)(2,1)}), bf16[32,8,16,128]{3,2,1,0:T(8,128)(2,1)S(1)}, u32[]{:S(2)}, u32[]{:S(2)}) %all-to-all-start.3) | async-done | bytes 1048608 | tf_op jit(solution)/shard_map/all_to_all | solution.py:313
  215.7 0.0 copy-start.1
  215.7 1.0 copy-done.1
  216.7 29.7 %shard_map.144 = bf16[16,64,64,128]{3,2,1,0:T(8,128)(2,1)} custom-call(bf16[8,4,2,4,16,128]{5,4,3,2,1,0:T(8,128)(2,1)} %bitcast.25, bf16[16,64,64,128]{3,2,1,0:T(8,128)(2,1)} %get-tuple-element.12.slope, bf16[256,256]{1,0:T(8,128)(2,1)} %mul.47.mix, bf16[128,512]{1,0:T(8,128)(2,1)} %constant.34.clone.z_adj, bf16[1024,512]{1,0:T(8,128)(2,1)} %constant.37.clone.y_inv, ...), custom_call_target="tpu_custom_call" | custom-call | tf_op jit(solution)/shard_map/pallas_call | solution.py:353
  (1 shorter events, 0.0 us)
Async XLA Ops:
  0.6 65.9 %copy-start.2 = (bf16[64,64]{1,0:T(8,128)(2,1)S(1)}, bf16[64,64]{1,0:T(8,128)(2,1)}, u32[]{:S(2)}) copy-start(bf16[64,64]{1,0:T(8,128)(2,1)} %param.16) | copy-start | bytes 24580
  63.4 29.5 %all-to-all-start.1 = ((bf16[32,8,16,128]{3,2,1,0:T(8,128)(2,1)}), bf16[32,8,16,128]{3,2,1,0:T(8,128)(2,1)S(1)}, u32[]{:S(2)}, u32[]{:S(2)}) async-start(bf16[32,8,16,128]{3,2,1,0:T(8,128)(2,1)} %bitcast.29), calls=%async_computation.1 | async-start | bytes 2097152 | tf_op jit(solution)/shard_map/all_to_all | solution.py:313
  92.9 1.0 copy-start
  186.2 29.5 %all-to-all-start.3 = ((bf16[32,8,16,128]{3,2,1,0:T(8,128)(2,1)}), bf16[32,8,16,128]{3,2,1,0:T(8,128)(2,1)S(1)}, u32[]{:S(2)}, u32[]{:S(2)}) async-start(bf16[32,8,16,128]{3,2,1,0:T(8,128)(2,1)} %bitcast.30), calls=%async_computation.3 | async-start | bytes 2097152 | tf_op jit(solution)/shard_map/all_to_all | solution.py:313
  215.7 1.0 copy-start.1
